TPU v7x, 256 devices: a whole 4x4x8 slice. The times are simulated.
256 devices in a mesh: wide: 32 (over x, y, core), narrow: 8 (over z).
Axes of the slice: x: 4, y: 4, z: 8, core: 2. Of those that a mesh axis runs over, the one named last changes fastest.
Arguments:
- sources: float32 [32, 8, 16, 2, 512], P('wide', 'narrow'), may hold values from -6 to 6
- schur_blocks: bfloat16 [32, 8, 2048, 2048], P('wide', 'narrow'), as said below
- scaling: float32 [32, 8, 2, 512], P('wide', 'narrow'), may hold values from 0.08 to 0.4
- coarse_basis: float32 [32, 8, 2, 2, 8, 512], P('wide', 'narrow'), may hold values from -0.09375 to 0.09375
- coarse_inverse: float32 [32, 80, 80], P('wide'), as said below
- face_sizes: int32 [32, 8, 2], P('wide', 'narrow'), may hold values from 0 to 512, as said below
- face_match: int32 [32, 8, 2, 512], P('wide', 'narrow'), may hold values from 0 to 511, as said below
- face_slots: int32 [32, 8, 4], P('wide', 'narrow'), may hold values from 0 to 3, each once within a row
- corner_slots: int32 [33, 9], replicated, may hold values from 0 to 319, as said below
Outputs:
- solution: float32 [32, 8, 16, 2, 512], P('wide', 'narrow')
- residual: float32 [32, 8, 16, 2, 512], P('wide', 'narrow')
Inputs may be any that keep to these rules, and one draw needn't show every extreme that they name: `face_sizes`: the east faces of the last wide index and the north faces of the last narrow index have 0 unknowns; every other face has 128 to 512, and some face has exactly 512. `face_match`: each block is a permutation of 0 to 511 that maps the positions below the size of the matching owned face onto themselves. `corner_slots`: distinct slots for distinct vertices; slot 319 is used. `schur_blocks`: each block is symmetric and positive definite. `coarse_inverse`: each block is symmetric and positive definite.
All inputs are finite; a program needn't handle non-finite values.
Results may differ from a plain program's by a relative error of at most 0.0052.
Values may be sent and summed in bfloat16 or wider, within the bound.
A program may use at most 64 MiB of HBM per device.

v0:
```python
import jax
import jax.numpy as jnp
from jax import lax
from jax.sharding import PartitionSpec as P

ITERS = 2
highest = lax.Precision.HIGHEST


def shifted(block, axis, distance):
    devices = range(lax.axis_size(axis))
    route = [(i - distance, i) for i in devices if i - distance in devices]
    return lax.ppermute(block, axis, route)


def body(
    sources,
    schur_blocks,
    scaling,
    coarse_basis,
    coarse_inverse,
    face_sizes,
    face_match,
    face_slots,
    corner_slots,
):
    wide_count = lax.axis_size("wide")
    wide_at = lax.axis_index("wide")
    narrow_at = lax.axis_index("narrow")
    nrhs_count = sources.shape[2]
    face_width = sources.shape[4]
    basis_count = coarse_basis.shape[4]
    block_order = coarse_inverse.shape[1]
    capacity = block_order // basis_count
    slot_count = capacity * wide_count
    places = lax.broadcasted_iota(jnp.int32, (2, face_width), 1)
    live_mask = (places < face_sizes[0, 0][:, None]).astype(jnp.float32)
    weights = scaling[0, 0] * live_mask
    vectors = coarse_basis[0, 0] * live_mask[:, None, None, :]
    forward = face_match[0, 0]
    source_rows = lax.broadcasted_iota(jnp.int32, (2, face_width, face_width), 1)
    match_table = (forward[:, None, :] == source_rows).astype(jnp.float32)
    match_narrow = match_table.astype(jnp.bfloat16)
    slot_table = (face_slots[0, 0][:, None] == jnp.arange(4, dtype=jnp.int32)[None, :]).astype(
        jnp.float32
    )
    matrix = schur_blocks[0, 0]
    square = lax.dynamic_slice(corner_slots, (wide_at, narrow_at), (2, 2))
    corner_ids = jnp.stack([square[1, 0], square[1, 1], square[0, 1], square[1, 1]])
    incidence = (corner_ids[:, None] == jnp.arange(slot_count, dtype=jnp.int32)[None, :]).astype(
        jnp.float32
    )
    inverse_block = coarse_inverse[0]
    initial = sources[0, 0] * live_mask[None]

    def finish(residual, solved_slots):
        local_values = jnp.dot(
            incidence, solved_slots, precision=highest, preferred_element_type=jnp.float32
        )
        local_values = local_values.reshape(2, 2, basis_count, nrhs_count)
        return weights[None] * residual + jnp.einsum(
            "femk,femr->rfk", vectors, local_values, precision=highest
        )

    def precondition(residual):
        partial_value = jnp.einsum("femk,rfk->femr", vectors, residual, precision=highest).reshape(
            4, basis_count * nrhs_count
        )
        dense_part = jnp.dot(
            incidence.T, partial_value, precision=highest, preferred_element_type=jnp.float32
        )
        owned_rows = lax.psum_scatter(dense_part, "wide", scatter_dimension=0, tiled=True)
        owner_block = lax.psum(owned_rows, "narrow").reshape(block_order, nrhs_count)
        solved = jnp.dot(
            inverse_block, owner_block, precision=highest, preferred_element_type=jnp.float32
        )
        all_solved = lax.all_gather(
            solved.reshape(capacity, basis_count * nrhs_count), "wide", axis=0, tiled=True
        )
        precond = finish(residual, all_solved)
        inner_value = lax.psum(jnp.sum(residual * precond, axis=(1, 2)), ("wide", "narrow"))
        return (precond, inner_value)

    residual = initial
    solution = jnp.zeros_like(initial)
    precond, inner_now = precondition(residual)
    direction = precond
    for iteration in range(ITERS):
        rounded = direction.astype(jnp.bfloat16)
        from_west = shifted(rounded[:, 0], "wide", 1)
        from_south = shifted(rounded[:, 1], "narrow", 1)
        west_face = jnp.dot(from_west, match_narrow[0], preferred_element_type=jnp.float32)
        south_face = jnp.dot(from_south, match_narrow[1], preferred_element_type=jnp.float32)
        stacked = jnp.stack(
            [
                rounded[:, 0].astype(jnp.float32),
                rounded[:, 1].astype(jnp.float32),
                west_face,
                south_face,
            ],
            axis=1,
        )
        slotted = jnp.einsum("rdk,ds->rsk", stacked, slot_table, precision=highest).astype(
            jnp.bfloat16
        )
        product = jnp.dot(
            slotted.reshape(nrhs_count, 4 * face_width), matrix, preferred_element_type=jnp.float32
        )
        by_face = jnp.einsum(
            "rsk,ds->rdk", product.reshape(nrhs_count, 4, face_width), slot_table, precision=highest
        )
        to_west = jnp.einsum("rk,mk->rm", by_face[:, 2], match_table[0], precision=highest)
        to_south = jnp.einsum("rk,mk->rm", by_face[:, 3], match_table[1], precision=highest)
        from_east = shifted(to_west, "wide", -1)
        from_north = shifted(to_south, "narrow", -1)
        summed_all = jnp.stack([by_face[:, 0] + from_east, by_face[:, 1] + from_north], axis=1)
        applied = summed_all * live_mask[None]
        curvature = lax.psum(jnp.sum(direction * applied, axis=(1, 2)), ("wide", "narrow"))
        step_size = inner_now / curvature
        solution = solution + step_size[:, None, None] * direction
        residual = residual - step_size[:, None, None] * applied
        if iteration + 1 < ITERS:
            precond, inner_new = precondition(residual)
            direction = precond + (inner_new / inner_now)[:, None, None] * direction
            inner_now = inner_new
    return (solution[None, None], residual[None, None])


def solution(mesh):
    placed = (
        P("wide", "narrow", None, None, None),
        P("wide", "narrow", None, None),
        P("wide", "narrow", None, None),
        P("wide", "narrow", None, None, None, None),
        P("wide", None, None),
        P("wide", "narrow", None),
        P("wide", "narrow", None, None),
        P("wide", "narrow", None),
        P(),
    )
    return jax.shard_map(
        body,
        mesh=mesh,
        in_specs=placed,
        out_specs=(P("wide", "narrow", None, None, None), P("wide", "narrow", None, None, None)),
        check_vma=False,
    )
```

profile of v0, /device:TPU:1, one launch (start us, length us, event | category | flops | bytes accessed | tf_op | source)
XLA Modules:
  0.0 640.1 jit_solution(5082868968421109135)
XLA Ops:
  10.6 2.1 pad_add_fusion
  16.4 110.0 %all-reduce.6.cloned.1.call-done = f32[320,128]{1,0:T(8,128)} async-done(((f32[320,128]{1,0:T(8,128)}), f32[320,128]{1,0:T(8,128)}) %all-reduce.6.cloned.1.call-update) | async-done | bytes 163856
  127.2 23.5 %psum.42 = f32[80,16]{1,0:T(8,128)S(1)} all-reduce(f32[80,16]{1,0:T(8,128)S(1)} %reshape.170), channel_id=1, replica_groups=mesh['wide'=32,'narrow'=8] {'narrow'}, use_global_device_ids=true, to_apply=%region_1.0 | all-reduce | flops 1280 | bytes 10240 | tf_op jit(solution)/shard_map/psum | solution.py:73
  151.1 30.1 %all-gather = f32[32,10,128]{2,1,0:T(8,128)S(1)} all-gather(f32[1,10,128]{2,1,0:T(8,128)S(1)} %reshape.179), channel_id=1, replica_groups=mesh['wide'=32,'narrow'=8] {'wide'}, dimensions={0}, use_global_device_ids=true | all-gather | bytes 168960 | tf_op jit(solution)/shard_map/all_gather | solution.py:77
  182.7 1.3 collective-permute-start.1
  185.3 12.3 %copy.57 = bf16[2048,2048]{1,0:T(8,128)(2,1)} copy(bf16[2048,2048]{0,1:T(8,128)(2,1)} %bitcast.206) | data formatting | bytes 16777216 | tf_op jit(solution)/shard_map/dot_general | solution.py:106
  197.6 2.6 collective-permute-start
  201.7 5.6 fusion.60
  208.9 1.3 collective-permute-start.3
  210.2 1.9 collective-permute-start.2
  212.1 2.1 collective-permute-done.3
  214.2 1.7 collective-permute-done.2
  216.1 78.5 %all-reduce.2 = (f32[16]{0:T(128)S(1)}, f32[16]{0:T(128)S(1)}) all-reduce(f32[16]{0:T(128)S(1)} %get-tuple-element.9, f32[16]{0:T(128)S(1)} %get-tuple-element.8), channel_id=1, replica_groups=mesh['wide'=32,'narrow'=8] {'wide','narrow'}, use_global_device_ids=true, to_apply=%region_3.0 | all-reduce | flops 32 | bytes 256 | tf_op jit(solution)/shard_map/psum | solution.py:81
  296.1 106.8 %all-reduce.8.cloned.1.call-done = f32[320,128]{1,0:T(8,128)} async-done(((f32[320,128]{1,0:T(8,128)}), f32[320,128]{1,0:T(8,128)}) %all-reduce.8.cloned.1.call-update) | async-done | bytes 163856
  403.7 23.5 %psum.45 = f32[80,16]{1,0:T(8,128)S(1)} all-reduce(f32[80,16]{1,0:T(8,128)S(1)} %reshape.175), channel_id=1, replica_groups=mesh['wide'=32,'narrow'=8] {'narrow'}, use_global_device_ids=true, to_apply=%region_7.0 | all-reduce | flops 1280 | bytes 10240 | tf_op jit(solution)/shard_map/psum | solution.py:73
  427.6 30.1 %all-gather.1 = f32[32,10,128]{2,1,0:T(8,128)S(1)} all-gather(f32[1,10,128]{2,1,0:T(8,128)S(1)} %reshape.181), channel_id=1, replica_groups=mesh['wide'=32,'narrow'=8] {'wide'}, dimensions={0}, use_global_device_ids=true | all-gather | bytes 168960 | tf_op jit(solution)/shard_map/all_gather | solution.py:77
  458.5 73.3 %psum.46 = f32[16]{0:T(128)S(1)} all-reduce(f32[16]{0:T(128)S(1)} %get-tuple-element.39), channel_id=1, replica_groups=mesh['wide'=32,'narrow'=8] {'wide','narrow'}, use_global_device_ids=true, to_apply=%region_9.0 | all-reduce | flops 16 | bytes 128 | tf_op jit(solution)/shard_map/psum | solution.py:81
  531.9 2.4 collective-permute-start.4
  534.4 3.9 collective-permute-start.5
  539.5 5.6 fusion.61
  546.7 1.3 collective-permute-start.7
  548.0 2.7 collective-permute-start.6
  551.6 1.6 collective-permute-done.6
  553.5 78.3 %psum.47 = f32[16]{0:T(128)S(1)} all-reduce(f32[16]{0:T(128)S(1)} %fusion.15), channel_id=1, replica_groups=mesh['wide'=32,'narrow'=8] {'wide','narrow'}, use_global_device_ids=true, to_apply=%region_11.0 | all-reduce | flops 16 | bytes 128 | tf_op jit(solution)/shard_map/psum | solution.py:118
  (79 shorter events, 22.3 us)
Async XLA Ops:
  7.2 143.6 %copy-start = (f32[1,80,80]{2,1,0:T(8,128)S(1)}, f32[1,80,80]{2,1,0:T(8,128)}, u32[]{:S(2)}) copy-start(f32[1,80,80]{2,1,0:T(8,128)} %param.13) | copy-start | bytes 76804
  7.2 119.2 %all-reduce.6.cloned.1.call-start = ((), (), s32[]{:S(2)}) async-start(), calls=%async_computation | async-start | bytes 327680
  13.7 389.2 %all-reduce.8.cloned.1.call-start = ((), (), s32[]{:S(2)}) async-start(), calls=%async_computation.1 | async-start | bytes 327680
  182.7 17.5 %collective-permute-start.1 = (bf16[16,512]{1,0:T(8,128)(2,1)S(1)}, bf16[16,512]{1,0:T(8,128)(2,1)S(1)}, u32[]{:S(2)}, u32[]{:S(2)}) collective-permute-start(bf16[16,512]{1,0:T(8,128)(2,1)S(1)} %get-tuple-element.30), channel_id=1, source_target_pairs={{0,1},{1,2},{2,3},{3,4},{4,5},{5,6},{6,7},{8,9},{9,10},{10,11},{11... | collective-permute-start | bytes 49160 | tf_op jit(solution)/shard_map/ppermute | solution.py:13
  185.3 16.0 %copy-start.3 = (s32[1,1,4]{2,1,0:T(1,128)S(1)}, s32[1,1,4]{2,1,0:T(1,128)}, u32[]{:S(2)}) copy-start(s32[1,1,4]{2,1,0:T(1,128)} %param.16) | copy-start | bytes 52
  197.6 18.4 %copy-start.1 = (f32[1,1,16,2,512]{4,3,2,1,0:T(2,128)S(1)}, f32[1,1,16,2,512]{4,3,2,1,0:T(2,128)}, u32[]{:S(2)}) copy-start(f32[1,1,16,2,512]{4,3,2,1,0:T(2,128)} %param.9) | copy-start | bytes 196612
  197.6 97.1 %copy-start.2 = (f32[1,1,2,2,8,512]{5,4,3,2,1,0:T(8,128)S(1)}, f32[1,1,2,2,8,512]{5,4,3,2,1,0:T(8,128)}, u32[]{:S(2)}) copy-start(f32[1,1,2,2,8,512]{5,4,3,2,1,0:T(8,128)} %param.12) | copy-start | bytes 196612
  197.6 3.4 collective-permute-start
  208.9 5.4 collective-permute-start.3
  210.2 5.8 collective-permute-start.2
  531.9 6.3 collective-permute-start.4
  534.4 4.5 collective-permute-start.5
  546.7 4.9 collective-permute-start.7
  548.0 5.2 collective-permute-start.6
Sparse Core Ops, SparseCore 0:
  13.8 112.5 all-reduce.5
  296.3 106.6 all-reduce.7
where the time goes:
time: 641 us; the launch traced here: 640 us
  blocking collectives  337 us (53%)
  waiting for transfers between devices  224 us (35%)
  matrix products  21.5 us (3%)
  local copies, waits for them, and re-layouts  18.9 us (3%)
  starting transfers between devices  17.5 us (3%)
  between operations  15 us (2%)
    unnamed x4, waiting for transfers between devices  217 us
    psum x2, blocking collectives, precondition(): lax.psum(jnp.sum(residual * precond, axis=(1, 2)), ('wide', 'narrow'))  152 us
    psum x1, blocking collectives, body(): lax.psum(jnp.sum(direction * applied, axis=(1, 2)), ('wide', 'narrow'))  78.3 us
    all_gather x2, blocking collectives, precondition(): lax.all_gather(solved.reshape(capacity, basis_count * nrhs_count), 'wide'...  60.2 us
    psum x2, blocking collectives, precondition(): lax.psum(owned_rows, 'narrow').reshape(block_order, nrhs_count)  47.1 us
    ppermute x8, starting transfers between devices, shifted(): return lax.ppermute(block, axis, route)  17.5 us
  transfers between devices with their start and end apart: 10, of which 8 were waited for; matrix products, arithmetic and copies ran while one was open for 2% of the time, Pallas kernels for 0%

commit v1 on v0

--- a/solution.py
+++ b/solution.py
@@ -1,3 +1,4 @@
+import functools
 import jax
 import jax.numpy as jnp
 from jax import lax
@@ -5,6 +6,15 @@
 
 ITERS = 2
 highest = lax.Precision.HIGHEST
+
+
+def _detail_vectors(x_part, link_axis, axis_id):
+    for dev in (link_axis, axis_id):
+        x_part = lax.psum(x_part, dev)
+    return x_part
+
+
+compute_words = functools.partial(_detail_vectors, link_axis="narrow", axis_id="wide")
 
 
 def shifted(block, axis, distance):
@@ -78,7 +88,7 @@
             solved.reshape(capacity, basis_count * nrhs_count), "wide", axis=0, tiled=True
         )
         precond = finish(residual, all_solved)
-        inner_value = lax.psum(jnp.sum(residual * precond, axis=(1, 2)), ("wide", "narrow"))
+        inner_value = compute_words(jnp.sum(residual * precond, axis=(1, 2)))
         return (precond, inner_value)
 
     residual = initial

time: 641 us -> 716 us (1.12)
  blocking collectives: 337 us -> 415 us
    psum x1 -> x2, blocking collectives: 78.3 us -> 154 us  [body(): lax.psum(jnp.sum(direction * applied, axis=(1, 2)), ('wide', 'narrow'))]
    psum x2 -> x4, blocking collectives: 152 us -> 154 us  [_detail_vectors(): x_part = lax.psum(x_part, dev)]
where the time goes in v1:
time: 716 us; the launch traced here: 715 us
  blocking collectives  415 us (58%)
  waiting for transfers between devices  222 us (31%)
  matrix products  21.5 us (3%)
  local copies, waits for them, and re-layouts  18.9 us (3%)
  starting transfers between devices  16.6 us (2%)
  between operations  15 us (2%)
    unnamed x4, waiting for transfers between devices  215 us
    psum x4, blocking collectives, _detail_vectors(): x_part = lax.psum(x_part, dev)  154 us
    psum x2, blocking collectives, body(): lax.psum(jnp.sum(direction * applied, axis=(1, 2)), ('wide', 'narrow'))  154 us
    all_gather x2, blocking collectives, precondition(): lax.all_gather(solved.reshape(capacity, basis_count * nrhs_count), 'wide'...  60.2 us
    psum x2, blocking collectives, precondition(): lax.psum(owned_rows, 'narrow').reshape(block_order, nrhs_count)  47.1 us
    ppermute x8, starting transfers between devices, shifted(): return lax.ppermute(block, axis, route)  16.5 us
  transfers between devices with their start and end apart: 10, of which 8 were waited for; matrix products, arithmetic and copies ran while one was open for 2% of the time, Pallas kernels for 0%

profile of v1, /device:TPU:1, one launch (start us, length us, event | category | flops | bytes accessed | tf_op | source)
XLA Modules:
  0.0 715.2 jit_solution(7133681904854708916)
XLA Ops:
  10.6 2.1 pad_add_fusion
  16.4 110.0 %all-reduce.5.cloned.1.call-done = f32[320,128]{1,0:T(8,128)} async-done(((f32[320,128]{1,0:T(8,128)}), f32[320,128]{1,0:T(8,128)}) %all-reduce.5.cloned.1.call-update) | async-done | bytes 163856
  127.2 23.5 %psum.56 = f32[80,16]{1,0:T(8,128)S(1)} all-reduce(f32[80,16]{1,0:T(8,128)S(1)} %reshape.170), channel_id=1, replica_groups=mesh['wide'=32,'narrow'=8] {'narrow'}, use_global_device_ids=true, to_apply=%region_1.0 | all-reduce | flops 1280 | bytes 10240 | tf_op jit(solution)/shard_map/psum | solution.py:83
  151.1 30.1 %all-gather = f32[32,10,128]{2,1,0:T(8,128)S(1)} all-gather(f32[1,10,128]{2,1,0:T(8,128)S(1)} %reshape.179), channel_id=1, replica_groups=mesh['wide'=32,'narrow'=8] {'wide'}, dimensions={0}, use_global_device_ids=true | all-gather | bytes 168960 | tf_op jit(solution)/shard_map/all_gather | solution.py:87
  185.3 12.3 %copy.57 = bf16[2048,2048]{1,0:T(8,128)(2,1)} copy(bf16[2048,2048]{0,1:T(8,128)(2,1)} %bitcast.206) | data formatting | bytes 16777216 | tf_op jit(solution)/shard_map/dot_general | solution.py:116
  197.6 2.6 collective-permute-start
  201.7 5.6 fusion.60
  210.2 1.9 collective-permute-start.2
  212.1 2.1 collective-permute-done.3
  214.2 1.7 collective-permute-done.2
  216.1 14.2 %psum.57 = f32[16]{0:T(128)S(1)} all-reduce(f32[16]{0:T(128)S(1)} %get-tuple-element.9), channel_id=1, replica_groups=mesh['wide'=32,'narrow'=8] {'narrow'}, use_global_device_ids=true, to_apply=%region_3.0 | all-reduce | flops 16 | bytes 128 | tf_op jit(solution)/shard_map/psum | solution.py:13
  230.4 78.1 %psum.59 = f32[16]{0:T(128)S(1)} all-reduce(f32[16]{0:T(128)S(1)} %get-tuple-element.8), channel_id=1, replica_groups=mesh['wide'=32,'narrow'=8] {'wide','narrow'}, use_global_device_ids=true, to_apply=%region_6.0 | all-reduce | flops 16 | bytes 128 | tf_op jit(solution)/shard_map/psum | solution.py:128
  308.5 62.9 %psum.58 = f32[16]{0:T(128)S(1)} all-reduce(f32[16]{0:T(128)S(1)} %psum.57), channel_id=1, replica_groups=mesh['wide'=32,'narrow'=8] {'wide'}, use_global_device_ids=true, to_apply=%region_4.0 | all-reduce | flops 16 | bytes 128 | tf_op jit(solution)/shard_map/psum | solution.py:13
  372.9 105.1 %all-reduce.7.cloned.1.call-done = f32[320,128]{1,0:T(8,128)} async-done(((f32[320,128]{1,0:T(8,128)}), f32[320,128]{1,0:T(8,128)}) %all-reduce.7.cloned.1.call-update) | async-done | bytes 163856
  478.8 23.5 %psum.60 = f32[80,16]{1,0:T(8,128)S(1)} all-reduce(f32[80,16]{1,0:T(8,128)S(1)} %reshape.175), channel_id=1, replica_groups=mesh['wide'=32,'narrow'=8] {'narrow'}, use_global_device_ids=true, to_apply=%region_8.0 | all-reduce | flops 1280 | bytes 10240 | tf_op jit(solution)/shard_map/psum | solution.py:83
  502.8 30.1 %all-gather.1 = f32[32,10,128]{2,1,0:T(8,128)S(1)} all-gather(f32[1,10,128]{2,1,0:T(8,128)S(1)} %reshape.181), channel_id=1, replica_groups=mesh['wide'=32,'narrow'=8] {'wide'}, dimensions={0}, use_global_device_ids=true | all-gather | bytes 168960 | tf_op jit(solution)/shard_map/all_gather | solution.py:87
  533.6 11.5 %psum.61 = f32[16]{0:T(128)S(1)} all-reduce(f32[16]{0:T(128)S(1)} %get-tuple-element.37), channel_id=1, replica_groups=mesh['wide'=32,'narrow'=8] {'narrow'}, use_global_device_ids=true, to_apply=%region_10.0 | all-reduce | flops 16 | bytes 128 | tf_op jit(solution)/shard_map/psum | solution.py:13
  545.0 65.8 %psum.62 = f32[16]{0:T(128)S(1)} all-reduce(f32[16]{0:T(128)S(1)} %psum.61), channel_id=1, replica_groups=mesh['wide'=32,'narrow'=8] {'wide'}, use_global_device_ids=true, to_apply=%region_11.0 | all-reduce | flops 16 | bytes 128 | tf_op jit(solution)/shard_map/psum | solution.py:13
  610.9 1.9 collective-permute-start.4
  612.8 2.9 collective-permute-start.5
  617.1 5.6 fusion.61
  625.6 3.3 collective-permute-start.6
  629.2 1.9 collective-permute-done.6
  631.3 75.5 %psum.63 = f32[16]{0:T(128)S(1)} all-reduce(f32[16]{0:T(128)S(1)} %fusion.15), channel_id=1, replica_groups=mesh['wide'=32,'narrow'=8] {'wide','narrow'}, use_global_device_ids=true, to_apply=%region_13.0 | all-reduce | flops 16 | bytes 128 | tf_op jit(solution)/shard_map/psum | solution.py:128
  (82 shorter events, 25.7 us)
Async XLA Ops:
  7.2 143.6 %copy-start = (f32[1,80,80]{2,1,0:T(8,128)S(1)}, f32[1,80,80]{2,1,0:T(8,128)}, u32[]{:S(2)}) copy-start(f32[1,80,80]{2,1,0:T(8,128)} %param.13) | copy-start | bytes 76804
  7.2 119.2 %all-reduce.5.cloned.1.call-start = ((), (), s32[]{:S(2)}) async-start(), calls=%async_computation | async-start | bytes 327680
  13.7 464.3 %all-reduce.7.cloned.1.call-start = ((), (), s32[]{:S(2)}) async-start(), calls=%async_computation.1 | async-start | bytes 327680
  182.7 17.5 %collective-permute-start.1 = (bf16[16,512]{1,0:T(8,128)(2,1)S(1)}, bf16[16,512]{1,0:T(8,128)(2,1)S(1)}, u32[]{:S(2)}, u32[]{:S(2)}) collective-permute-start(bf16[16,512]{1,0:T(8,128)(2,1)S(1)} %get-tuple-element.28), channel_id=1, source_target_pairs={{0,1},{1,2},{2,3},{3,4},{4,5},{5,6},{6,7},{8,9},{9,10},{10,11},{11... | collective-permute-start | bytes 49160 | tf_op jit(solution)/shard_map/ppermute | solution.py:23
  185.3 16.0 %copy-start.3 = (s32[1,1,4]{2,1,0:T(1,128)S(1)}, s32[1,1,4]{2,1,0:T(1,128)}, u32[]{:S(2)}) copy-start(s32[1,1,4]{2,1,0:T(1,128)} %param.16) | copy-start | bytes 52
  197.6 18.4 %copy-start.1 = (f32[1,1,16,2,512]{4,3,2,1,0:T(2,128)S(1)}, f32[1,1,16,2,512]{4,3,2,1,0:T(2,128)}, u32[]{:S(2)}) copy-start(f32[1,1,16,2,512]{4,3,2,1,0:T(2,128)} %param.9) | copy-start | bytes 196612
  197.6 173.8 %copy-start.2 = (f32[1,1,2,2,8,512]{5,4,3,2,1,0:T(8,128)S(1)}, f32[1,1,2,2,8,512]{5,4,3,2,1,0:T(8,128)}, u32[]{:S(2)}) copy-start(f32[1,1,2,2,8,512]{5,4,3,2,1,0:T(8,128)} %param.12) | copy-start | bytes 196612
  197.6 3.4 collective-permute-start
  208.9 5.4 collective-permute-start.3
  210.2 5.8 collective-permute-start.2
  610.9 4.9 collective-permute-start.4
  612.8 3.6 collective-permute-start.5
  624.2 4.9 collective-permute-start.7
  625.6 5.5 collective-permute-start.6
Sparse Core Ops, SparseCore 0:
  13.8 112.5 all-reduce.4
  373.0 104.9 all-reduce.6
